TPU v7x, 32 devices: a whole 2x2x4 slice. The times are simulated.
32 devices in a mesh: dom: 8 (over z, x), rep: 4 (over y, core).
Axes of the slice: x: 2, y: 2, z: 4, core: 2. Of those that a mesh axis runs over, the one named last changes fastest.
Arguments:
- inputs: bfloat16 [4, 2048, 768], P('rep', 'dom'), may hold values from -6 to 6
- cotangent: bfloat16 [4, 2048, 576], P('rep', 'dom'), may hold values from -6 to 6
- conv_one: bfloat16 [2, 64, 128], replicated, may hold values from -1 to 1
- conv_two: bfloat16 [2, 64, 128], replicated, may hold values from -1 to 1
- mix_weight: bfloat16 [3, 64, 64], replicated, may hold values from -2 to 2
- send_rows: int32 [8, 8, 128], P('dom'), may hold values from 0 to 255, as said below
- counts: int32 [8, 8], P('dom'), may hold values from 0 to 128, as said below
- tile_cols: int32 [16, 12], P('dom'), may hold values from 0 to 9, as said below
- tile_vals: bfloat16 [16, 12, 128, 128], P('dom'), may hold values from -0.15625 to 0.15625
Outputs:
- output: bfloat16 [4, 2048, 576], P('rep', 'dom')
- grad_input: bfloat16 [4, 2048, 768], P('rep', 'dom')
- grad_conv_one: float32 [2, 64, 128], replicated
- grad_conv_two: float32 [2, 64, 128], replicated
- grad_mix: float32 [3, 64, 64], replicated
Inputs may be any that keep to these rules, and one draw needn't show every extreme that they name: `send_rows`: rows of the source partition; entries in slots at or beyond counts are arbitrary rows. `counts`: zero for a partition with itself; every partition fills one block completely. `tile_cols`: entries below 2 are own row tiles, entry 2 + q is the block from partition q. Each partition's tiles name each of its own row tiles once and the block from the partition before it; which other blocks are named differs from partition to partition.
All inputs are finite; a program needn't handle non-finite values.
Results may differ from a plain program's by a relative error of at most 0.0075.
Values may be sent and summed in bfloat16 or wider, within the bound.
A program may use at most 128 MiB of HBM per device.

v0:
```python
import functools
import math

import jax
import jax.numpy as jnp
from jax import lax
from jax.experimental import pallas as pl
from jax.experimental.pallas import tpu as pltpu
from jax.sharding import PartitionSpec as P

F32 = jnp.float32
BF16 = jnp.bfloat16
BLK = 128
VM = pl.BlockSpec(memory_space=pltpu.VMEM)
SM = pl.BlockSpec(memory_space=pltpu.SMEM)
LIMIT = pltpu.CompilerParams(vmem_limit_bytes=56 * 1024 * 1024)


def dot(a, b):
    return jnp.dot(a, b, preferred_element_type=F32)


def dot_t0(a, b):
    return lax.dot_general(a, b, (((0,), (0,)), ((), ())), preferred_element_type=F32)


def dot_t1(a, b):
    return lax.dot_general(a, b, (((1,), (1,)), ((), ())), preferred_element_type=F32)


def pair(k):
    return slice(k * 128, (k + 1) * 128)


def window2(k):
    return slice(k * 128, (k + 2) * 128)


def block_map(weight_ref, index, out_ref):
    c = weight_ref.shape[1]
    w = weight_ref[index]
    out_ref[...] = jnp.zeros(out_ref.shape, BF16)
    out_ref[0:c, 0:c] = w
    out_ref[c : 2 * c, c : 2 * c] = w


def band_blocks(dilation):
    if dilation == 1:
        return ((0, 1, 0), (0, 2, 1), (1, 2, 0), (1, 3, 1))
    return ((0, 0, 0), (0, 1, 1), (1, 2, 0), (1, 3, 1))


def band_map(conv_ref, dilation, out_ref):
    c = conv_ref.shape[1]
    out_ref[...] = jnp.zeros(out_ref.shape, BF16)
    for tap, i, o in band_blocks(dilation):
        w = conv_ref[tap]
        rows = slice(i * c, (i + 1) * c)
        out_ref[rows, o * c : (o + 1) * c] = w[:, :c]
        out_ref[rows, (o + 2) * c : (o + 3) * c] = w[:, c:]


def band_grad(total, dilation, out_ref):
    c = out_ref.shape[1]
    for tap in range(2):
        for half in range(2):
            acc = None
            for t, i, o in band_blocks(dilation):
                if t != tap:
                    continue
                col = (o + 2 * half) * c
                part = total[i * c : (i + 1) * c, col : col + c]
                acc = part if acc is None else acc + part
            out_ref[tap, :, half * c : (half + 1) * c] = acc


def activations(pre):
    filt = jnp.tanh(pre[:, :128])
    gates = 0.5 * jnp.tanh(0.5 * pre[:, 128:]) + 0.5
    return filt, gates


def earlier(ref, k):
    if k == 0:
        x = ref[:, 0:128]
        return jnp.concatenate([jnp.zeros_like(x), x], axis=1)
    return ref[:, window2(k - 1)]


def build_tiles(cols_ref, vals_ref, acc_ref, dense_ref):
    rtiles, slots = vals_ref.shape[0], vals_ref.shape[1]
    ctiles = dense_ref.shape[1] // BLK
    for r in range(rtiles):
        acc_ref[...] = jnp.zeros(acc_ref.shape, F32)
        for j in range(slots):
            c = cols_ref[r, j]
            acc_ref[c] = acc_ref[c] + vals_ref[r, j].astype(F32)
        for c in range(ctiles):
            dense_ref[r * BLK : (r + 1) * BLK, c * BLK : (c + 1) * BLK] = acc_ref[c].astype(BF16)


def build_picks(send_ref, counts_ref, picks_ref):
    parts = send_ref.shape[0]
    nodes = picks_ref.shape[0]
    lane = lax.broadcasted_iota(jnp.int32, (1, BLK), 1)
    rows = lax.broadcasted_iota(jnp.int32, (nodes, BLK), 0)
    for q in range(parts):
        wanted = jnp.where(lane < counts_ref[0, q], send_ref[q : q + 1, :], -1)
        hit = rows == wanted
        picks_ref[:, q * BLK : (q + 1) * BLK] = jnp.where(hit, 1.0, 0.0).astype(BF16)


def prepare_body(cot_ref, mix_ref, send_ref, counts_ref, cols_ref, vals_ref,
                 dense_ref, picks_ref, cot_out, base_ref, pieces_ref,
                 acc_ref, map_ref, g_ref):
    nodes = cot_ref.shape[0]
    c = mix_ref.shape[1]
    build_tiles(cols_ref, vals_ref, acc_ref, dense_ref)
    build_picks(send_ref, counts_ref, picks_ref)
    wide = cot_ref[...].astype(F32)
    wide = jnp.concatenate([jnp.zeros((nodes, c), F32), wide], axis=1).astype(BF16)
    cot_out[...] = wide
    pairs = cot_out.shape[1] // 128
    block_map(mix_ref, 2, map_ref)
    m = map_ref[...]
    for k in range(pairs):
        g_ref[:, pair(k)] = dot_t1(cot_out[:, pair(k)], m).astype(BF16)
    block_map(mix_ref, 1, map_ref)
    m = map_ref[...]
    g = g_ref[...]
    pieces_ref[...] = dot_t0(dense_ref[:, nodes:], g).astype(BF16)
    base_ref[...] = dot_t0(dense_ref[:, :nodes], g)
    for k in range(pairs):
        base_ref[:, pair(k)] += dot_t1(cot_out[:, pair(k)], m)


def forward_body(x_ref, conv1_ref, conv2_ref, picks_ref, first_ref, hidden_ref, halo_ref,
                 band_ref):
    pairs = x_ref.shape[1] // 128
    band_map(conv1_ref, 1, band_ref)
    b = band_ref[...]
    for k in range(pairs):
        filt, gates = activations(dot(earlier(x_ref, k), b))
        first_ref[:, pair(k)] = (filt * gates).astype(BF16)
    band_map(conv2_ref, 2, band_ref)
    b = band_ref[...]
    for k in range(1, pairs):
        filt, gates = activations(dot(earlier(first_ref, k), b))
        hidden_ref[:, pair(k - 1)] = (filt * gates).astype(BF16)
    halo_ref[...] = dot_t0(picks_ref[...], hidden_ref[...]).astype(BF16)


def back_hop_body(arrived_ref, picks_ref, dense_ref, base_ref, cot_ref, mix_ref,
                  next_base_ref, pieces_ref, map_ref):
    nodes = cot_ref.shape[0]
    pairs = cot_ref.shape[1] // 128
    g = (base_ref[...] + dot(picks_ref[...], arrived_ref[...])).astype(BF16)
    pieces_ref[...] = dot_t0(dense_ref[:, nodes:], g).astype(BF16)
    next_base_ref[...] = dot_t0(dense_ref[:, :nodes], g)
    block_map(mix_ref, 0, map_ref)
    m = map_ref[...]
    for k in range(pairs):
        next_base_ref[:, pair(k)] += dot_t1(cot_ref[:, pair(k)], m)


def hop_body(arrived_ref, picks_ref, dense_ref, hidden_ref, hop_ref, halo_ref):
    nodes = hidden_ref.shape[0]
    total = dot(dense_ref[:, :nodes], hidden_ref[...])
    total = total + dot(dense_ref[:, nodes:], arrived_ref[...])
    hop_ref[...] = total.astype(BF16)
    halo_ref[...] = dot_t0(picks_ref[...], hop_ref[...]).astype(BF16)


def gate_grad(pre, up):
    filt, gates = activations(pre)
    d_filt = up * gates * (1.0 - filt * filt)
    d_gate = up * filt * gates * (1.0 - gates)
    return jnp.concatenate([d_filt, d_gate], axis=1).astype(BF16)


def backward_body(arrived_ref, picks_ref, base_ref, x_ref, first_ref, cot_ref,
                  conv1_ref, conv2_ref, grad_ref, g1_ref, g2_ref,
                  band_ref, up_ref, mid_ref):
    pairs = x_ref.shape[1] // 128
    up_ref[...] = base_ref[...] + dot(picks_ref[...], arrived_ref[...])
    band_map(conv2_ref, 2, band_ref)
    b = band_ref[...]
    total = None
    carry = None
    for k in range(1, pairs):
        both = earlier(first_ref, k)
        d = gate_grad(dot(both, b), up_ref[:, pair(k - 1)])
        part = dot_t0(both, d)
        total = part if total is None else total + part
        back = dot_t1(d, b)
        low = back[:, :128] if carry is None else carry + back[:, :128]
        mid_ref[:, pair(k - 1)] = low.astype(BF16)
        carry = back[:, 128:]
    mid_ref[:, pair(pairs - 1)] = carry.astype(BF16)
    band_grad(total, 2, g2_ref)
    band_map(conv1_ref, 1, band_ref)
    b = band_ref[...]
    total = None
    carry = None
    for k in range(pairs):
        both = earlier(x_ref, k)
        d = gate_grad(dot(both, b), mid_ref[:, pair(k)].astype(F32))
        part = dot_t0(both, d)
        total = part if total is None else total + part
        back = dot_t1(d, b)
        if k > 0:
            low = carry + back[:, :128]
            if k > 1:
                low = low + cot_ref[:, pair(k - 2)].astype(F32)
            grad_ref[:, pair(k - 1)] = low.astype(BF16)
        carry = back[:, 128:]
    last = carry + cot_ref[:, pair(pairs - 2)].astype(F32)
    grad_ref[:, pair(pairs - 1)] = last.astype(BF16)
    band_grad(total, 1, g1_ref)


def finish_body(arrived_ref, dense_ref, hidden_ref, hop_ref, x_ref, cot_ref, mix_ref,
                out_ref, gm_ref, map0, map1, map2, second_ref, wide_ref):
    nodes = hidden_ref.shape[0]
    c = mix_ref.shape[1]
    pairs = hidden_ref.shape[1] // 128
    total = dot(dense_ref[:, :nodes], hop_ref[...])
    total = total + dot(dense_ref[:, nodes:], arrived_ref[...])
    second_ref[...] = total.astype(BF16)
    terms = (hidden_ref, hop_ref, second_ref)
    maps = (map0, map1, map2)
    for i in range(3):
        block_map(mix_ref, i, maps[i])
    for k in range(pairs):
        acc = x_ref[:, pair(k + 1)].astype(F32)
        for term, m in zip(terms, maps):
            acc = acc + dot(term[:, pair(k)], m[...])
        wide_ref[:, pair(k)] = acc
    out_ref[...] = wide_ref[:, c:].astype(BF16)
    for i, term in enumerate(terms):
        acc = None
        for k in range(pairs):
            part = dot_t0(term[:, pair(k)], cot_ref[:, pair(k)])
            acc = part if acc is None else acc + part
        gm_ref[i] = acc[:c, :c] + acc[c:, c:]


def call(body, outs, scratch, ins, specs=None, name=None, flops=0, moved=0):
    return pl.pallas_call(
        body,
        out_shape=[jax.ShapeDtypeStruct(s, d) for s, d in outs],
        in_specs=specs or [VM] * len(ins),
        out_specs=[VM] * len(outs),
        scratch_shapes=[pltpu.VMEM(s, d) for s, d in scratch],
        compiler_params=LIMIT,
        cost_estimate=pl.CostEstimate(flops=flops, bytes_accessed=moved, transcendentals=0),
        name=name,
    )(*ins)


def total_over(values, axes, devices):
    size = values.size
    per = -(-size // devices)
    flat = jnp.pad(values, (0, per * devices - size)).reshape(devices, per)
    got = lax.all_to_all(flat, axes, split_axis=0, concat_axis=0, tiled=True)
    mine = jnp.sum(got, axis=0)
    spread = jnp.broadcast_to(mine[None], (devices, per))
    back = lax.all_to_all(spread, axes, split_axis=0, concat_axis=0, tiled=True)
    return back.reshape(-1)[:size]


def shards(inputs, cotangent, conv_one, conv_two, mix_weight, send_rows, counts, tile_cols,
           tile_vals):
    windows, nodes, flat = inputs.shape
    channels = mix_weight.shape[1]
    parts = lax.axis_size("dom")
    reps = lax.axis_size("rep")
    kept = flat // channels - 3
    wide = flat - 2 * channels
    halo = parts * BLK
    x = inputs[0]
    cot = cotangent[0]
    hop_flops = 4 * nodes * halo * wide
    moved = 2 * halo * wide * 2

    def exchange(v):
        return lax.all_to_all(v, "dom", split_axis=0, concat_axis=0, tiled=True)

    dense, picks, cot_wide, base, pieces = call(
        prepare_body,
        [((nodes, nodes + halo), BF16), ((nodes, halo), BF16), ((nodes, wide), BF16),
         ((nodes, wide), F32), ((halo, wide), BF16)],
        [((parts + nodes // BLK, BLK, BLK), F32), ((128, 128), BF16), ((nodes, wide), BF16)],
        (cot, mix_weight, send_rows[0], counts, tile_cols, tile_vals),
        [VM, VM, VM, SM, SM, VM], "prepare", hop_flops, moved)
    arrived_back = exchange(pieces)
    first, hidden, out_halo = call(
        forward_body,
        [((nodes, flat), BF16), ((nodes, wide), BF16), ((halo, wide), BF16)],
        [((256, 256), BF16)],
        (x, conv_one, conv_two, picks), None, "forward", hop_flops, moved)
    arrived = exchange(out_halo)
    base, pieces = call(
        back_hop_body,
        [((nodes, wide), F32), ((halo, wide), BF16)],
        [((128, 128), BF16)],
        (arrived_back, picks, dense, base, cot_wide, mix_weight), None, "back_hop",
        hop_flops, moved)
    arrived_back = exchange(pieces)
    hop, out_halo = call(
        hop_body,
        [((nodes, wide), BF16), ((halo, wide), BF16)], [],
        (arrived, picks, dense, hidden), None, "hop", hop_flops, moved)
    arrived = exchange(out_halo)
    grad_input, g1, g2 = call(
        backward_body,
        [((nodes, flat), BF16), (conv_one.shape, F32), (conv_two.shape, F32)],
        [((256, 256), BF16), ((nodes, wide), F32), ((nodes, flat), BF16)],
        (arrived_back, picks, base, x, first, cot_wide, conv_one, conv_two), None, "backward",
        hop_flops, moved)
    output, gm = call(
        finish_body,
        [((nodes, kept * channels), BF16), (mix_weight.shape, F32)],
        [((128, 128), BF16)] * 3 + [((nodes, wide), BF16), ((nodes, wide), F32)],
        (arrived, dense, hidden, hop, x, cot_wide, mix_weight), None, "finish",
        hop_flops, moved)
    scaling = math.sqrt(float(windows * reps * nodes * parts * kept))
    packed = jnp.concatenate([g1.reshape(-1), g2.reshape(-1), gm.reshape(-1)])
    packed = total_over(packed, ("dom", "rep"), parts * reps) / scaling
    n1, n2 = g1.size, g2.size
    return (
        output[None],
        grad_input[None],
        packed[:n1].reshape(g1.shape),
        packed[n1 : n1 + n2].reshape(g2.shape),
        packed[n1 + n2 :].reshape(gm.shape),
    )


def solution(mesh):
    placed = (
        P("rep", "dom", None),
        P("rep", "dom", None),
        P(),
        P(),
        P(),
        P("dom", None, None),
        P("dom", None),
        P("dom", None),
        P("dom", None, None, None),
    )
    return jax.shard_map(
        shards,
        mesh=mesh,
        in_specs=placed,
        out_specs=(P("rep", "dom", None), P("rep", "dom", None), P(), P(), P()),
        check_vma=False,
    )
```

profile of v0, /device:TPU:0, one launch (start us, length us, event | category | flops | bytes accessed | tf_op | source)
XLA Modules:
  0.0 190.0 jit_solution(15712188681031225384)
XLA Ops:
  0.6 1.9 copy.20
  2.5 4.2 %prepare.1 = (bf16[256,1280]{1,0:T(8,128)(2,1)}, bf16[256,1024]{1,0:T(8,128)(2,1)}, bf16[256,640]{1,0:T(8,128)(2,1)}, f32[256,640]{1,0:T(8,128)}, bf16[1024,640]{1,0:T(8,128)(2,1)}) custom-call(bf16[256,576]{1,0:T(8,128)(2,1)} %bitcast.32, bf16[3,64,64]{2,1,0:T(8,128)(2,1)} %mix_ref.5, s32[8,128]{1,0:T(8,128)} %bitcast.38, s32[1,8]{1,0:T(1,128)} %counts_ref.1, ...), custom_call_target="tpu_custom_call" | custom-call | flops 671088640 | bytes 2621440 | tf_op jit(solution)/shard_map/prepare/pallas_call | solution.py:249
  6.7 3.4 %forward.1 = (bf16[256,768]{1,0:T(8,128)(2,1)}, bf16[256,640]{1,0:T(8,128)(2,1)}, bf16[1024,640]{1,0:T(8,128)(2,1)}) custom-call(bf16[256,768]{1,0:T(8,128)(2,1)} %bitcast.23, bf16[2,64,128]{2,1,0:T(8,128)(2,1)} %conv1_ref.3, bf16[2,64,128]{2,1,0:T(8,128)(2,1)} %conv2_ref.3, bf16[256,1024]{1,0:T(8,128)(2,1)} %get-tuple-element.22.picks_ref), custom_call_target="tpu_custom_call" | custom-call | flops 671088640 | bytes 2621440 | tf_op jit(solution)/shard_map/forward/pallas_call | solution.py:249
  10.1 38.7 %all_to_all.59 = bf16[8,128,640]{2,1,0:T(8,128)(2,1)} all-to-all(bf16[8,128,640]{2,1,0:T(8,128)(2,1)} %bitcast.28), channel_id=1, replica_groups=mesh['dom'=8,'rep'=4] {'dom'}, dimensions={0} | all-to-all | bytes 2621440 | tf_op jit(solution)/shard_map/all_to_all | solution.py:287
  48.8 3.6 %all-to-all-start.2 = ((bf16[8,128,640]{2,1,0:T(8,128)(2,1)}), bf16[8,128,640]{2,1,0:T(8,128)(2,1)S(1)}, u32[]{:S(2)}, u32[]{:S(2)}) async-start(bf16[8,128,640]{2,1,0:T(8,128)(2,1)} %bitcast.8), calls=%async_computation.2 | async-start | bytes 2621440 | tf_op jit(solution)/shard_map/all_to_all | solution.py:287
  52.4 4.0 %hop.1 = (bf16[256,640]{1,0:T(8,128)(2,1)}, bf16[1024,640]{1,0:T(8,128)(2,1)}) custom-call(bf16[1024,640]{1,0:T(8,128)(2,1)} %bitcast.22, bf16[256,1024]{1,0:T(8,128)(2,1)} %get-tuple-element.22.picks_ref, bf16[256,1280]{1,0:T(8,128)(2,1)} %get-tuple-element.24.dense_ref, bf16[256,640]{1,0:T(8,128)(2,1)} %get-tuple-element.25.hidden_ref), custom_call_target="tpu_custom_call" | custom-call | flops 671088640 | bytes 2621440 | tf_op jit(solution)/shard_map/hop/pallas_call | solution.py:249
  56.4 27.0 %all-to-all-done.2 = bf16[8,128,640]{2,1,0:T(8,128)(2,1)S(1)} async-done(((bf16[8,128,640]{2,1,0:T(8,128)(2,1)}), bf16[8,128,640]{2,1,0:T(8,128)(2,1)S(1)}, u32[]{:S(2)}, u32[]{:S(2)}) %all-to-all-start.2) | async-done | bytes 1310752 | tf_op jit(solution)/shard_map/all_to_all | solution.py:287
  83.5 0.0 copy-start.2
  83.5 1.1 copy-done.2
  84.5 3.6 %all-to-all-start.1 = ((bf16[8,128,640]{2,1,0:T(8,128)(2,1)}), bf16[8,128,640]{2,1,0:T(8,128)(2,1)S(1)}, u32[]{:S(2)}, u32[]{:S(2)}) async-start(bf16[8,128,640]{2,1,0:T(8,128)(2,1)} %bitcast.27), calls=%async_computation.1 | async-start | bytes 2621440 | tf_op jit(solution)/shard_map/all_to_all | solution.py:287
  88.1 4.3 %back_hop.1 = (f32[256,640]{1,0:T(8,128)}, bf16[1024,640]{1,0:T(8,128)(2,1)}) custom-call(bf16[1024,640]{1,0:T(8,128)(2,1)} %bitcast.21, bf16[256,1024]{1,0:T(8,128)(2,1)} %get-tuple-element.22.picks_ref, bf16[256,1280]{1,0:T(8,128)(2,1)} %get-tuple-element.24.dense_ref, f32[256,640]{1,0:T(8,128)} %get-tuple-element.31.base_ref, ...), custom_call_target="tpu_custom_call" | custom-call | flops 671088640 | bytes 2621440 | tf_op jit(solution)/shard_map/back_hop/pallas_call | solution.py:249
  92.4 27.3 %all-to-all-done.1 = bf16[8,128,640]{2,1,0:T(8,128)(2,1)S(1)} async-done(((bf16[8,128,640]{2,1,0:T(8,128)(2,1)}), bf16[8,128,640]{2,1,0:T(8,128)(2,1)S(1)}, u32[]{:S(2)}, u32[]{:S(2)}) %all-to-all-start.1) | async-done | bytes 1310752 | tf_op jit(solution)/shard_map/all_to_all | solution.py:287
  119.7 0.0 copy-start.1
  119.7 1.1 copy-done.1
  120.7 3.6 %all-to-all-start.3 = ((bf16[8,128,640]{2,1,0:T(8,128)(2,1)}), bf16[8,128,640]{2,1,0:T(8,128)(2,1)S(1)}, u32[]{:S(2)}, u32[]{:S(2)}) async-start(bf16[8,128,640]{2,1,0:T(8,128)(2,1)} %bitcast.26), calls=%async_computation.3 | async-start | bytes 2621440 | tf_op jit(solution)/shard_map/all_to_all | solution.py:287
  124.4 3.8 %finish.1 = (bf16[256,576]{1,0:T(8,128)(2,1)}, f32[3,64,64]{2,1,0:T(8,128)}) custom-call(bf16[1024,640]{1,0:T(8,128)(2,1)} %bitcast.20, bf16[256,1280]{1,0:T(8,128)(2,1)} %get-tuple-element.24.dense_ref, bf16[256,640]{1,0:T(8,128)(2,1)} %get-tuple-element.25.hidden_ref, bf16[256,640]{1,0:T(8,128)(2,1)} %get-tuple-element.27.hop_ref, ...), custom_call_target="tpu_custom_call" | custom-call | flops 671088640 | bytes 2621440 | tf_op jit(solution)/shard_map/finish/pallas_call | solution.py:249
  128.2 1.0 reshape.55
  129.2 26.8 %all-to-all-done.3 = bf16[8,128,640]{2,1,0:T(8,128)(2,1)S(1)} async-done(((bf16[8,128,640]{2,1,0:T(8,128)(2,1)}), bf16[8,128,640]{2,1,0:T(8,128)(2,1)S(1)}, u32[]{:S(2)}, u32[]{:S(2)}) %all-to-all-start.3) | async-done | bytes 1310752 | tf_op jit(solution)/shard_map/all_to_all | solution.py:287
  155.9 1.1 copy-done
  157.0 5.6 %backward.1 = (bf16[256,768]{1,0:T(8,128)(2,1)}, f32[2,64,128]{2,1,0:T(8,128)}, f32[2,64,128]{2,1,0:T(8,128)}) custom-call(bf16[1024,640]{1,0:T(8,128)(2,1)} %bitcast.19, bf16[256,1024]{1,0:T(8,128)(2,1)} %get-tuple-element.22.picks_ref, f32[256,640]{1,0:T(8,128)} %get-tuple-element.33.base_ref, bf16[256,768]{1,0:T(8,128)(2,1)} %bitcast.25, ...), custom_call_target="tpu_custom_call" | custom-call | flops 671088640 | bytes 2621440 | tf_op jit(solution)/shard_map/backward/pallas_call | solution.py:249
  162.6 0.9 pad_maximum_fusion
  163.5 12.2 %all_to_all.60 = f32[32,1,1408]{2,1,0:T(1,128)S(1)} all-to-all(f32[32,1,1408]{2,1,0:T(1,128)S(1)} %bitcast.29), channel_id=1, replica_groups=mesh['dom'=8,'rep'=4] {'dom','rep'}, dimensions={0} | all-to-all | bytes 360448 | tf_op jit(solution)/shard_map/all_to_all | solution.py:265
  175.7 0.1 reduce_sum.9
  175.9 0.8 broadcast_in_dim.14
  176.6 2.6 %all-to-all-start.5 = ((f32[32,1,1408]{2,1,0:T(1,128)}), f32[32,1,1408]{2,1,0:T(1,128)S(1)}, u32[]{:S(2)}, u32[]{:S(2)}) async-start(f32[32,1,1408]{2,1,0:T(1,128)} %broadcast_in_dim.14), calls=%async_computation.5 | async-start | bytes 360448 | tf_op jit(solution)/shard_map/all_to_all | solution.py:268
  179.2 0.0 copy-done.3
  179.2 0.9 copy.22
  180.1 7.8 %all-to-all-done.5 = f32[32,1,1408]{2,1,0:T(1,128)S(1)} async-done(((f32[32,1,1408]{2,1,0:T(1,128)}), f32[32,1,1408]{2,1,0:T(1,128)S(1)}, u32[]{:S(2)}, u32[]{:S(2)}) %all-to-all-start.5) | async-done | bytes 180256 | tf_op jit(solution)/shard_map/all_to_all | solution.py:268
  187.9 0.6 fusion
  188.5 0.7 fusion.1
  189.2 0.1 div.13
  189.3 0.6 slice.15
  (2 shorter events, 0.0 us)
Async XLA Ops:
  48.8 34.6 %all-to-all-start.2 = ((bf16[8,128,640]{2,1,0:T(8,128)(2,1)}), bf16[8,128,640]{2,1,0:T(8,128)(2,1)S(1)}, u32[]{:S(2)}, u32[]{:S(2)}) async-start(bf16[8,128,640]{2,1,0:T(8,128)(2,1)} %bitcast.8), calls=%async_computation.2 | async-start | bytes 2621440 | tf_op jit(solution)/shard_map/all_to_all | solution.py:287
  83.5 1.1 copy-start.2
  84.5 35.2 %all-to-all-start.1 = ((bf16[8,128,640]{2,1,0:T(8,128)(2,1)}), bf16[8,128,640]{2,1,0:T(8,128)(2,1)S(1)}, u32[]{:S(2)}, u32[]{:S(2)}) async-start(bf16[8,128,640]{2,1,0:T(8,128)(2,1)} %bitcast.27), calls=%async_computation.1 | async-start | bytes 2621440 | tf_op jit(solution)/shard_map/all_to_all | solution.py:287
  119.7 1.1 copy-start.1
  120.7 35.2 %all-to-all-start.3 = ((bf16[8,128,640]{2,1,0:T(8,128)(2,1)}), bf16[8,128,640]{2,1,0:T(8,128)(2,1)S(1)}, u32[]{:S(2)}, u32[]{:S(2)}) async-start(bf16[8,128,640]{2,1,0:T(8,128)(2,1)} %bitcast.26), calls=%async_computation.3 | async-start | bytes 2621440 | tf_op jit(solution)/shard_map/all_to_all | solution.py:287
  155.9 1.1 copy-start
  162.6 16.6 %copy-start.3 = (bf16[256,576]{1,0:T(8,128)(2,1)S(1)}, bf16[256,576]{1,0:T(8,128)(2,1)}, u32[]{:S(2)}) copy-start(bf16[256,576]{1,0:T(8,128)(2,1)} %get-tuple-element.29) | copy-start | bytes 884740
  176.6 11.3 %all-to-all-start.5 = ((f32[32,1,1408]{2,1,0:T(1,128)}), f32[32,1,1408]{2,1,0:T(1,128)S(1)}, u32[]{:S(2)}, u32[]{:S(2)}) async-start(f32[32,1,1408]{2,1,0:T(1,128)} %broadcast_in_dim.14), calls=%async_computation.5 | async-start | bytes 360448 | tf_op jit(solution)/shard_map/all_to_all | solution.py:268
where the time goes:
time: 191 us; the launch traced here: 190 us
  waiting for transfers between devices  88.9 us (47%)
  blocking collectives  51 us (27%)
  Pallas kernels  25.3 us (13%)
  starting transfers between devices  13.4 us (7%)
  local copies, waits for them, and re-layouts  9.08 us (5%)
    all_to_all x3, waiting for transfers between devices, exchange(): return lax.all_to_all(v, 'dom', split_axis=0, concat_axis=0, tiled=True)  81 us
    all_to_all x1, blocking collectives, exchange(): return lax.all_to_all(v, 'dom', split_axis=0, concat_axis=0, tiled=True)  38.7 us
    pallas_call x6, Pallas kernels, call(): pl.pallas_call(body, out_shape=[jax.ShapeDtypeStruct(s, d) for s, d in ou...  25.3 us
    all_to_all x1, blocking collectives, total_over(): got = lax.all_to_all(flat, axes, split_axis=0, concat_axis=0, tiled=True)  12.2 us
    all_to_all x3, starting transfers between devices, exchange(): return lax.all_to_all(v, 'dom', split_axis=0, concat_axis=0, tiled=True)  10.8 us
    all_to_all x1, waiting for transfers between devices, total_over(): back = lax.all_to_all(spread, axes, split_axis=0, concat_axis=0, tiled=True)  7.84 us
    unnamed x10, local copies, waits for them, and re-layouts  5.93 us
  transfers between devices with their start and end apart: 4, of which 4 were waited for; matrix products, arithmetic and copies ran while one was open for 1% of the time, Pallas kernels for 6%

commit v1 on v0

--- a/solution.py
+++ b/solution.py
@@ -114,6 +114,7 @@
                  dense_ref, picks_ref, cot_out, base_ref, pieces_ref,
                  acc_ref, map_ref, g_ref):
     nodes = cot_ref.shape[0]
+    parts = send_ref.shape[0]
     c = mix_ref.shape[1]
     build_tiles(cols_ref, vals_ref, acc_ref, dense_ref)
     build_picks(send_ref, counts_ref, picks_ref)
@@ -128,14 +129,27 @@
     block_map(mix_ref, 1, map_ref)
     m = map_ref[...]
     g = g_ref[...]
-    pieces_ref[...] = dot_t0(dense_ref[:, nodes:], g).astype(BF16)
+    pack_rows(g, dense_ref, nodes, parts, pieces_ref)
     base_ref[...] = dot_t0(dense_ref[:, :nodes], g)
     for k in range(pairs):
         base_ref[:, pair(k)] += dot_t1(cot_out[:, pair(k)], m)
 
 
-def forward_body(x_ref, conv1_ref, conv2_ref, picks_ref, first_ref, hidden_ref, halo_ref,
-                 band_ref):
+def pack_rows(values, table_ref, start, parts, out_ref):
+    flipped = values.astype(F32).T.astype(BF16)
+    for q in range(parts):
+        table = table_ref[:, start + q * BLK : start + (q + 1) * BLK]
+        out_ref[q] = dot(flipped, table).astype(BF16)
+
+
+def from_blocks(total, table_ref, start, parts, arrived_ref):
+    for q in range(parts):
+        table = table_ref[:, start + q * BLK : start + (q + 1) * BLK]
+        total = total + dot_t1(table, arrived_ref[q])
+    return total
+
+
+def forward_part(x_ref, conv1_ref, conv2_ref, first_ref, hidden_ref, band_ref):
     pairs = x_ref.shape[1] // 128
     band_map(conv1_ref, 1, band_ref)
     b = band_ref[...]
@@ -147,28 +161,6 @@
     for k in range(1, pairs):
         filt, gates = activations(dot(earlier(first_ref, k), b))
         hidden_ref[:, pair(k - 1)] = (filt * gates).astype(BF16)
-    halo_ref[...] = dot_t0(picks_ref[...], hidden_ref[...]).astype(BF16)
-
-
-def back_hop_body(arrived_ref, picks_ref, dense_ref, base_ref, cot_ref, mix_ref,
-                  next_base_ref, pieces_ref, map_ref):
-    nodes = cot_ref.shape[0]
-    pairs = cot_ref.shape[1] // 128
-    g = (base_ref[...] + dot(picks_ref[...], arrived_ref[...])).astype(BF16)
-    pieces_ref[...] = dot_t0(dense_ref[:, nodes:], g).astype(BF16)
-    next_base_ref[...] = dot_t0(dense_ref[:, :nodes], g)
-    block_map(mix_ref, 0, map_ref)
-    m = map_ref[...]
-    for k in range(pairs):
-        next_base_ref[:, pair(k)] += dot_t1(cot_ref[:, pair(k)], m)
-
-
-def hop_body(arrived_ref, picks_ref, dense_ref, hidden_ref, hop_ref, halo_ref):
-    nodes = hidden_ref.shape[0]
-    total = dot(dense_ref[:, :nodes], hidden_ref[...])
-    total = total + dot(dense_ref[:, nodes:], arrived_ref[...])
-    hop_ref[...] = total.astype(BF16)
-    halo_ref[...] = dot_t0(picks_ref[...], hop_ref[...]).astype(BF16)
 
 
 def gate_grad(pre, up):
@@ -178,11 +170,9 @@
     return jnp.concatenate([d_filt, d_gate], axis=1).astype(BF16)
 
 
-def backward_body(arrived_ref, picks_ref, base_ref, x_ref, first_ref, cot_ref,
-                  conv1_ref, conv2_ref, grad_ref, g1_ref, g2_ref,
+def backward_part(x_ref, first_ref, cot_ref, conv1_ref, conv2_ref, grad_ref, g1_ref, g2_ref,
                   band_ref, up_ref, mid_ref):
     pairs = x_ref.shape[1] // 128
-    up_ref[...] = base_ref[...] + dot(picks_ref[...], arrived_ref[...])
     band_map(conv2_ref, 2, band_ref)
     b = band_ref[...]
     total = None
@@ -219,14 +209,10 @@
     band_grad(total, 1, g1_ref)
 
 
-def finish_body(arrived_ref, dense_ref, hidden_ref, hop_ref, x_ref, cot_ref, mix_ref,
-                out_ref, gm_ref, map0, map1, map2, second_ref, wide_ref):
-    nodes = hidden_ref.shape[0]
+def finish_part(hidden_ref, hop_ref, second_ref, x_ref, cot_ref, mix_ref,
+                out_ref, gm_ref, map0, map1, map2, wide_ref):
     c = mix_ref.shape[1]
     pairs = hidden_ref.shape[1] // 128
-    total = dot(dense_ref[:, :nodes], hop_ref[...])
-    total = total + dot(dense_ref[:, nodes:], arrived_ref[...])
-    second_ref[...] = total.astype(BF16)
     terms = (hidden_ref, hop_ref, second_ref)
     maps = (map0, map1, map2)
     for i in range(3):
@@ -245,28 +231,173 @@
         gm_ref[i] = acc[:c, :c] + acc[c:, c:]
 
 
-def call(body, outs, scratch, ins, specs=None, name=None, flops=0, moved=0):
-    return pl.pallas_call(
-        body,
-        out_shape=[jax.ShapeDtypeStruct(s, d) for s, d in outs],
-        in_specs=specs or [VM] * len(ins),
-        out_specs=[VM] * len(outs),
-        scratch_shapes=[pltpu.VMEM(s, d) for s, d in scratch],
-        compiler_params=LIMIT,
-        cost_estimate=pl.CostEstimate(flops=flops, bytes_accessed=moved, transcendentals=0),
-        name=name,
-    )(*ins)
-
-
-def total_over(values, axes, devices):
-    size = values.size
-    per = -(-size // devices)
-    flat = jnp.pad(values, (0, per * devices - size)).reshape(devices, per)
-    got = lax.all_to_all(flat, axes, split_axis=0, concat_axis=0, tiled=True)
-    mine = jnp.sum(got, axis=0)
-    spread = jnp.broadcast_to(mine[None], (devices, per))
-    back = lax.all_to_all(spread, axes, split_axis=0, concat_axis=0, tiled=True)
-    return back.reshape(-1)[:size]
+def main_body(parts, reps, scale,
+              x_ref, cot_ref, conv1_ref, conv2_ref, mix_ref, dense_ref, picks_ref, base_ref,
+              pieces_ref,
+              out_ref, grad_ref, o1_ref, o2_ref, om_ref,
+              first_ref, hidden_ref, hop_ref, second_ref, up_ref, mid_ref, band_ref,
+              map0, map1, map2, g1_ref, g2_ref, gm_ref,
+              send1, send2, send3, recv0, recv1, recv2, recv3,
+              pack_ref, got_ref, part_ref, reps_ref, sums_ref,
+              ssem, rsem, asem, arsem, bsem, brsem):
+    me = lax.axis_index("dom")
+    mine = lax.axis_index("rep")
+    nodes = x_ref.shape[0]
+    c = mix_ref.shape[1]
+    pairs = cot_ref.shape[1] // 128
+    feats = cot_ref.shape[1]
+
+    barrier = pltpu.get_barrier_semaphore()
+    for o in range(1, parts):
+        pl.semaphore_signal(barrier, inc=1, device_id={"dom": lax.rem(me + o, parts)},
+                            device_id_type=pl.DeviceIdType.MESH)
+    for o in range(1, reps):
+        pl.semaphore_signal(barrier, inc=1, device_id={"rep": lax.rem(mine + o, reps)},
+                            device_id_type=pl.DeviceIdType.MESH)
+    pl.semaphore_wait(barrier, parts - 1 + reps - 1)
+
+    def copies(level, src, dst):
+        made = []
+        for o in range(1, parts):
+            peer = lax.rem(me + o, parts)
+            made.append(pltpu.make_async_remote_copy(
+                src_ref=src.at[peer, pl.ds(c, feats - c)],
+                dst_ref=dst.at[me, pl.ds(c, feats - c)],
+                send_sem=ssem.at[level, o],
+                recv_sem=rsem.at[level, o],
+                device_id={"dom": peer},
+                device_id_type=pl.DeviceIdType.MESH,
+            ))
+        for m in made:
+            m.start()
+        return made
+
+    def arrive(made):
+        for m in made:
+            m.wait_recv()
+
+    round0 = copies(0, pieces_ref, recv0)
+    for buf in (recv0, recv1, recv2, recv3):
+        buf[:, 0:c, :] = jnp.zeros((parts, c, BLK), BF16)
+        buf[me] = jnp.zeros((feats, BLK), BF16)
+
+    forward_part(x_ref, conv1_ref, conv2_ref, first_ref, hidden_ref, band_ref)
+    pack_rows(hidden_ref[...], picks_ref, 0, parts, send1)
+    round1 = copies(1, send1, recv1)
+
+    arrive(round0)
+    g = from_blocks(base_ref[...], picks_ref, 0, parts, recv0).astype(BF16)
+    pack_rows(g, dense_ref, nodes, parts, send2)
+    round2 = copies(2, send2, recv2)
+    up_ref[...] = dot_t0(dense_ref[:, :nodes], g)
+    block_map(mix_ref, 0, map0)
+    for k in range(pairs):
+        up_ref[:, pair(k)] += dot_t1(cot_ref[:, pair(k)], map0[...])
+
+    own = dot(dense_ref[:, :nodes], hidden_ref[...])
+    arrive(round1)
+    hop_ref[...] = from_blocks(own, dense_ref, nodes, parts, recv1).astype(BF16)
+    pack_rows(hop_ref[...], picks_ref, 0, parts, send3)
+    round3 = copies(3, send3, recv3)
+
+    arrive(round2)
+    up_ref[...] = from_blocks(up_ref[...], picks_ref, 0, parts, recv2)
+    backward_part(x_ref, first_ref, cot_ref, conv1_ref, conv2_ref, grad_ref, g1_ref, g2_ref,
+                  band_ref, up_ref, mid_ref)
+
+    own = dot(dense_ref[:, :nodes], hop_ref[...])
+    arrive(round3)
+    second_ref[...] = from_blocks(own, dense_ref, nodes, parts, recv3).astype(BF16)
+    finish_part(hidden_ref, hop_ref, second_ref, x_ref, cot_ref, mix_ref, out_ref, gm_ref,
+                map0, map1, map2, up_ref)
+    for made in (round0, round1, round2, round3):
+        for m in made:
+            m.wait_send()
+
+    per = pack_ref.shape[1]
+    flat = pack_ref
+    flat[...] = jnp.zeros(flat.shape, F32)
+
+    def put(first_row, value):
+        rows = value.shape[0]
+        done = 0
+        while done < rows:
+            slot, at = divmod(first_row + done, per)
+            step = min(per - at, rows - done)
+            flat[slot, at : at + step, :] = value[done : done + step]
+            done += step
+
+    put(0, g1_ref[0])
+    put(c, g1_ref[1])
+    put(2 * c, g2_ref[0])
+    put(3 * c, g2_ref[1])
+    put(4 * c, jnp.concatenate([gm_ref[0], gm_ref[1]], axis=1))
+    put(5 * c, jnp.concatenate([gm_ref[2], jnp.zeros((c, c), F32)], axis=1))
+
+    scatter = []
+    for o in range(1, parts):
+        peer = lax.rem(me + o, parts)
+        scatter.append(pltpu.make_async_remote_copy(
+            src_ref=pack_ref.at[peer], dst_ref=got_ref.at[me],
+            send_sem=asem.at[0, o], recv_sem=arsem.at[0, o],
+            device_id={"dom": peer}, device_id_type=pl.DeviceIdType.MESH))
+    for m in scatter:
+        m.start()
+    got_ref[me] = pack_ref[me]
+    arrive(scatter)
+    total = got_ref[0]
+    for q in range(1, parts):
+        total = total + got_ref[q]
+    part_ref[...] = total
+    around = []
+    for o in range(1, reps):
+        peer = lax.rem(mine + o, reps)
+        around.append(pltpu.make_async_remote_copy(
+            src_ref=part_ref, dst_ref=reps_ref.at[mine],
+            send_sem=bsem.at[o], recv_sem=brsem.at[o],
+            device_id={"rep": peer}, device_id_type=pl.DeviceIdType.MESH))
+    for m in around:
+        m.start()
+    reps_ref[mine] = total
+    arrive(around)
+    total = reps_ref[0]
+    for q in range(1, reps):
+        total = total + reps_ref[q]
+    for m in around:
+        m.wait_send()
+    part_ref[...] = total * (1.0 / scale)
+    final = []
+    for o in range(1, parts):
+        peer = lax.rem(me + o, parts)
+        final.append(pltpu.make_async_remote_copy(
+            src_ref=part_ref, dst_ref=sums_ref.at[me],
+            send_sem=asem.at[1, o], recv_sem=arsem.at[1, o],
+            device_id={"dom": peer}, device_id_type=pl.DeviceIdType.MESH))
+    for m in final:
+        m.start()
+    sums_ref[me] = part_ref[...]
+    arrive(final)
+
+    def take(first_row, rows):
+        found = []
+        done = 0
+        while done < rows:
+            slot, at = divmod(first_row + done, per)
+            step = min(per - at, rows - done)
+            found.append(sums_ref[slot, at : at + step, :])
+            done += step
+        return jnp.concatenate(found, axis=0) if len(found) > 1 else found[0]
+
+    o1_ref[0] = take(0, c)
+    o1_ref[1] = take(c, c)
+    o2_ref[0] = take(2 * c, c)
+    o2_ref[1] = take(3 * c, c)
+    both = take(4 * c, c)
+    om_ref[0] = both[:, :c]
+    om_ref[1] = both[:, c:]
+    om_ref[2] = take(5 * c, c)[:, :c]
+    for m in scatter + final:
+        m.wait_send()
 
 
 def shards(inputs, cotangent, conv_one, conv_two, mix_weight, send_rows, counts, tile_cols,
@@ -278,63 +409,45 @@
     kept = flat // channels - 3
     wide = flat - 2 * channels
     halo = parts * BLK
-    x = inputs[0]
-    cot = cotangent[0]
-    hop_flops = 4 * nodes * halo * wide
-    moved = 2 * halo * wide * 2
-
-    def exchange(v):
-        return lax.all_to_all(v, "dom", split_axis=0, concat_axis=0, tiled=True)
-
-    dense, picks, cot_wide, base, pieces = call(
+    blocks = (parts, wide, BLK)
+    prepared = [((nodes, nodes + halo), BF16), ((nodes, halo), BF16), ((nodes, wide), BF16),
+                ((nodes, wide), F32), (blocks, BF16)]
+    dense, picks, cot_wide, base, pieces = pl.pallas_call(
         prepare_body,
-        [((nodes, nodes + halo), BF16), ((nodes, halo), BF16), ((nodes, wide), BF16),
-         ((nodes, wide), F32), ((halo, wide), BF16)],
-        [((parts + nodes // BLK, BLK, BLK), F32), ((128, 128), BF16), ((nodes, wide), BF16)],
-        (cot, mix_weight, send_rows[0], counts, tile_cols, tile_vals),
-        [VM, VM, VM, SM, SM, VM], "prepare", hop_flops, moved)
-    arrived_back = exchange(pieces)
-    first, hidden, out_halo = call(
-        forward_body,
-        [((nodes, flat), BF16), ((nodes, wide), BF16), ((halo, wide), BF16)],
-        [((256, 256), BF16)],
-        (x, conv_one, conv_two, picks), None, "forward", hop_flops, moved)
-    arrived = exchange(out_halo)
-    base, pieces = call(
-        back_hop_body,
-        [((nodes, wide), F32), ((halo, wide), BF16)],
-        [((128, 128), BF16)],
-        (arrived_back, picks, dense, base, cot_wide, mix_weight), None, "back_hop",
-        hop_flops, moved)
-    arrived_back = exchange(pieces)
-    hop, out_halo = call(
-        hop_body,
-        [((nodes, wide), BF16), ((halo, wide), BF16)], [],
-        (arrived, picks, dense, hidden), None, "hop", hop_flops, moved)
-    arrived = exchange(out_halo)
-    grad_input, g1, g2 = call(
-        backward_body,
-        [((nodes, flat), BF16), (conv_one.shape, F32), (conv_two.shape, F32)],
-        [((256, 256), BF16), ((nodes, wide), F32), ((nodes, flat), BF16)],
-        (arrived_back, picks, base, x, first, cot_wide, conv_one, conv_two), None, "backward",
-        hop_flops, moved)
-    output, gm = call(
-        finish_body,
-        [((nodes, kept * channels), BF16), (mix_weight.shape, F32)],
-        [((128, 128), BF16)] * 3 + [((nodes, wide), BF16), ((nodes, wide), F32)],
-        (arrived, dense, hidden, hop, x, cot_wide, mix_weight), None, "finish",
-        hop_flops, moved)
+        out_shape=[jax.ShapeDtypeStruct(s, d) for s, d in prepared],
+        in_specs=[VM, VM, VM, SM, SM, VM],
+        out_specs=[VM] * 5,
+        scratch_shapes=[pltpu.VMEM((parts + nodes // BLK, BLK, BLK), F32),
+                        pltpu.VMEM((128, 128), BF16), pltpu.VMEM((nodes, wide), BF16)],
+        compiler_params=LIMIT,
+        name="prepare",
+    )(cotangent[0], mix_weight, send_rows[0], counts, tile_cols, tile_vals)
     scaling = math.sqrt(float(windows * reps * nodes * parts * kept))
-    packed = jnp.concatenate([g1.reshape(-1), g2.reshape(-1), gm.reshape(-1)])
-    packed = total_over(packed, ("dom", "rep"), parts * reps) / scaling
-    n1, n2 = g1.size, g2.size
-    return (
-        output[None],
-        grad_input[None],
-        packed[:n1].reshape(g1.shape),
-        packed[n1 : n1 + n2].reshape(g2.shape),
-        packed[n1 + n2 :].reshape(gm.shape),
-    )
+    unit = 8 * parts
+    per = -(-6 * channels // unit) * unit // parts
+    results = [((nodes, kept * channels), BF16), ((nodes, flat), BF16), (conv_one.shape, F32),
+               (conv_two.shape, F32), (mix_weight.shape, F32)]
+    scratch = [((nodes, flat), BF16), ((nodes, wide), BF16), ((nodes, wide), BF16),
+               ((nodes, wide), BF16), ((nodes, wide), F32), ((nodes, flat), BF16),
+               ((256, 256), BF16), ((128, 128), BF16), ((128, 128), BF16), ((128, 128), BF16),
+               (conv_one.shape, F32), (conv_two.shape, F32), (mix_weight.shape, F32)]
+    scratch += [(blocks, BF16)] * 7
+    scratch += [((parts, per, BLK), F32), ((parts, per, BLK), F32), ((per, BLK), F32),
+                ((reps, per, BLK), F32), ((parts, per, BLK), F32)]
+    dma = pltpu.SemaphoreType.DMA
+    output, grad_input, g1, g2, gm = pl.pallas_call(
+        functools.partial(main_body, parts, reps, scaling),
+        out_shape=[jax.ShapeDtypeStruct(s, d) for s, d in results],
+        in_specs=[VM] * 9,
+        out_specs=[VM] * 5,
+        scratch_shapes=[pltpu.VMEM(s, d) for s, d in scratch]
+        + [dma((4, parts)), dma((4, parts)), dma((2, parts)), dma((2, parts)), dma((reps,)),
+           dma((reps,))],
+        compiler_params=pltpu.CompilerParams(
+            vmem_limit_bytes=60 * 1024 * 1024, collective_id=0, has_side_effects=True),
+        name="layer",
+    )(inputs[0], cot_wide, conv_one, conv_two, mix_weight, dense, picks, base, pieces)
+    return output[None], grad_input[None], g1, g2, gm
 
 
 def solution(mesh):

time: 191 us -> 143 us (0.75)
  Pallas kernels: 25.3 us -> 134 us
  waiting for transfers between devices: 88.9 us -> 0 us
  blocking collectives: 51 us -> 0 us
  starting transfers between devices: 13.4 us -> 0 us
    pallas_call x6 -> x2, Pallas kernels: 25.3 us -> 134 us  [the longest x1 130 us: shards(): pl.pallas_call(functools.partial(main_body, parts, reps, scaling), out_sh...]
    all_to_all x4 -> x0, waiting for transfers between devices: 88.9 us -> none  [the longest x3 81 us: exchange(): return lax.all_to_all(v, 'dom', split_axis=0, concat_axis=0, tiled=True)]
    all_to_all x2 -> x0, blocking collectives: 51 us -> none  [the longest x1 38.7 us: exchange(): return lax.all_to_all(v, 'dom', split_axis=0, concat_axis=0, tiled=True)]
    all_to_all x4 -> x0, starting transfers between devices: 13.4 us -> none  [the longest x3 10.8 us: exchange(): return lax.all_to_all(v, 'dom', split_axis=0, concat_axis=0, tiled=True)]
    unnamed x10 -> x12, local copies, waits for them, and re-layouts: 5.93 us -> 7.42 us
  transfers between devices with their start and end apart: 4 -> 0, of which waited for: 4 -> 0; matrix products, arithmetic and copies ran while one was open for 1% -> 0% of each run, Pallas kernels for 6% -> 0%
where the time goes in v1:
time: 143 us; the launch traced here: 142 us
  Pallas kernels  134 us (94%)
  local copies, waits for them, and re-layouts  7.42 us (5%)
    pallas_call x1, Pallas kernels, shards(): pl.pallas_call(functools.partial(main_body, parts, reps, scaling), out_sh...  130 us
    unnamed x12, local copies, waits for them, and re-layouts  7.42 us
    pallas_call x1, Pallas kernels, shards(): pl.pallas_call(prepare_body, out_shape=[jax.ShapeDtypeStruct(s, d) for s,...  4.57 us

profile of v1, /device:TPU:0, one launch (start us, length us, event | category | flops | bytes accessed | tf_op | source)
XLA Modules:
  0.0 142.4 jit_solution(17753533476584952878)
XLA Ops:
  0.6 1.9 %copy.14 = bf16[1,256,576]{2,1,0:T(8,128)(2,1)} copy(bf16[1,256,576]{1,2,0:T(8,128)(2,1)} %param.10) | data formatting | bytes 589824 | tf_op args[1]
  2.5 4.6 %prepare.1 = (bf16[256,1280]{1,0:T(8,128)(2,1)}, bf16[256,1024]{1,0:T(8,128)(2,1)}, bf16[256,640]{1,0:T(8,128)(2,1)}, f32[256,640]{1,0:T(8,128)}, bf16[8,640,128]{2,1,0:T(8,128)(2,1)}) custom-call(bf16[256,576]{1,0:T(8,128)(2,1)} %bitcast.5, bf16[3,64,64]{2,1,0:T(8,128)(2,1)} %mix_ref.3, s32[8,128]{1,0:T(8,128)} %bitcast.9, s32[1,8]{1,0:T(1,128)} %counts_ref.1, ...), custom_call_target="tpu_custom_call" | custom-call | tf_op jit(solution)/shard_map/prepare/pallas_call | solution.py:415
  7.1 129.8 %layer.1 = (bf16[256,576]{1,0:T(8,128)(2,1)}, bf16[256,768]{1,0:T(8,128)(2,1)}, f32[2,64,128]{2,1,0:T(8,128)}, f32[2,64,128]{2,1,0:T(8,128)}, f32[3,64,64]{2,1,0:T(8,128)}) custom-call(bf16[256,768]{1,0:T(8,128)(2,1)} %bitcast.7, bf16[256,640]{1,0:T(8,128)(2,1)} %get-tuple-element.15.cot_ref, bf16[2,64,128]{2,1,0:T(8,128)(2,1)} %conv1_ref.1, ...), custom_call_target="tpu_custom_call" | custom-call | tf_op jit(solution)/shard_map/layer/pallas_call | solution.py:438
  136.8 0.0 copy-start.2
  136.8 0.0 copy-start.1
  136.8 0.0 copy-start
  136.9 1.9 %copy.15 = bf16[1,256,576]{1,2,0:T(8,128)(2,1)} copy(bf16[1,256,576]{2,1,0:T(8,128)(2,1)} %bitcast.8) | data formatting | bytes 589824
  138.7 1.8 %copy.20 = bf16[1,256,768]{2,1,0:T(8,128)(2,1)} copy(bf16[1,256,768]{2,1,0:T(8,128)(2,1)} %bitcast.6) | data formatting | bytes 786432
  140.5 0.0 copy-done.2
  140.5 0.6 copy.21
  141.1 0.0 copy-done.1
  141.1 0.6 copy.22
  141.8 0.0 copy-done
  141.8 0.6 copy.23
Async XLA Ops:
  136.8 3.7 %copy-start.2 = (f32[2,64,128]{2,1,0:T(8,128)S(1)}, f32[2,64,128]{2,1,0:T(8,128)}, u32[]{:S(2)}) copy-start(f32[2,64,128]{2,1,0:T(8,128)} %get-tuple-element.37) | copy-start | bytes 196612
  136.8 4.3 %copy-start.1 = (f32[2,64,128]{2,1,0:T(8,128)S(1)}, f32[2,64,128]{2,1,0:T(8,128)}, u32[]{:S(2)}) copy-start(f32[2,64,128]{2,1,0:T(8,128)} %get-tuple-element.38) | copy-start | bytes 196612
  136.8 4.9 %copy-start = (f32[3,64,64]{2,1,0:T(8,128)S(1)}, f32[3,64,64]{2,1,0:T(8,128)}, u32[]{:S(2)}) copy-start(f32[3,64,64]{2,1,0:T(8,128)} %get-tuple-element.39) | copy-start | bytes 147460

commit v2 on v1

--- a/solution.py
+++ b/solution.py
@@ -113,12 +113,12 @@
 def prepare_body(cot_ref, mix_ref, send_ref, counts_ref, cols_ref, vals_ref,
                  dense_ref, picks_ref, cot_out, base_ref, pieces_ref,
                  acc_ref, map_ref, g_ref):
-    nodes = cot_ref.shape[0]
+    nodes = cot_ref.shape[1]
     parts = send_ref.shape[0]
     c = mix_ref.shape[1]
     build_tiles(cols_ref, vals_ref, acc_ref, dense_ref)
     build_picks(send_ref, counts_ref, picks_ref)
-    wide = cot_ref[...].astype(F32)
+    wide = cot_ref[...].astype(F32).T
     wide = jnp.concatenate([jnp.zeros((nodes, c), F32), wide], axis=1).astype(BF16)
     cot_out[...] = wide
     pairs = cot_out.shape[1] // 128
@@ -209,26 +209,24 @@
     band_grad(total, 1, g1_ref)
 
 
-def finish_part(hidden_ref, hop_ref, second_ref, x_ref, cot_ref, mix_ref,
-                out_ref, gm_ref, map0, map1, map2, wide_ref):
+def mix_grad(term_ref, cot_ref, c):
+    acc = None
+    for k in range(cot_ref.shape[1] // 128):
+        part = dot_t0(term_ref[:, pair(k)], cot_ref[:, pair(k)])
+        acc = part if acc is None else acc + part
+    return acc[:c, :c] + acc[c:, c:]
+
+
+def early_part(hidden_ref, hop_ref, x_ref, cot_ref, mix_ref, gm_ref, map0, map1, wide_ref):
     c = mix_ref.shape[1]
-    pairs = hidden_ref.shape[1] // 128
-    terms = (hidden_ref, hop_ref, second_ref)
-    maps = (map0, map1, map2)
-    for i in range(3):
-        block_map(mix_ref, i, maps[i])
-    for k in range(pairs):
+    block_map(mix_ref, 0, map0)
+    block_map(mix_ref, 1, map1)
+    for k in range(cot_ref.shape[1] // 128):
         acc = x_ref[:, pair(k + 1)].astype(F32)
-        for term, m in zip(terms, maps):
-            acc = acc + dot(term[:, pair(k)], m[...])
-        wide_ref[:, pair(k)] = acc
-    out_ref[...] = wide_ref[:, c:].astype(BF16)
-    for i, term in enumerate(terms):
-        acc = None
-        for k in range(pairs):
-            part = dot_t0(term[:, pair(k)], cot_ref[:, pair(k)])
-            acc = part if acc is None else acc + part
-        gm_ref[i] = acc[:c, :c] + acc[c:, c:]
+        acc = acc + dot(hidden_ref[:, pair(k)], map0[...])
+        wide_ref[:, pair(k)] = acc + dot(hop_ref[:, pair(k)], map1[...])
+    gm_ref[0] = mix_grad(hidden_ref, cot_ref, c)
+    gm_ref[1] = mix_grad(hop_ref, cot_ref, c)
 
 
 def main_body(parts, reps, scale,
@@ -237,7 +235,7 @@
               out_ref, grad_ref, o1_ref, o2_ref, om_ref,
               first_ref, hidden_ref, hop_ref, second_ref, up_ref, mid_ref, band_ref,
               map0, map1, map2, g1_ref, g2_ref, gm_ref,
-              send1, send2, send3, recv0, recv1, recv2, recv3,
+              wide_ref, send1, send2, send3, recv0, recv1, recv2, recv3,
               pack_ref, got_ref, part_ref, reps_ref, sums_ref,
               ssem, rsem, asem, arsem, bsem, brsem):
     me = lax.axis_index("dom")
@@ -258,7 +256,7 @@
 
     def copies(level, src, dst):
         made = []
-        for o in range(1, parts):
+        for o in sorted(range(1, parts), key=lambda o: abs(2 * o - parts)):
             peer = lax.rem(me + o, parts)
             made.append(pltpu.make_async_remote_copy(
                 src_ref=src.at[peer, pl.ds(c, feats - c)],
@@ -305,14 +303,12 @@
     backward_part(x_ref, first_ref, cot_ref, conv1_ref, conv2_ref, grad_ref, g1_ref, g2_ref,
                   band_ref, up_ref, mid_ref)
 
+    early_part(hidden_ref, hop_ref, x_ref, cot_ref, mix_ref, gm_ref, map0, map1, wide_ref)
+    block_map(mix_ref, 2, map2)
     own = dot(dense_ref[:, :nodes], hop_ref[...])
     arrive(round3)
     second_ref[...] = from_blocks(own, dense_ref, nodes, parts, recv3).astype(BF16)
-    finish_part(hidden_ref, hop_ref, second_ref, x_ref, cot_ref, mix_ref, out_ref, gm_ref,
-                map0, map1, map2, up_ref)
-    for made in (round0, round1, round2, round3):
-        for m in made:
-            m.wait_send()
+    gm_ref[2] = mix_grad(second_ref, cot_ref, c)
 
     per = pack_ref.shape[1]
     flat = pack_ref
@@ -343,6 +339,9 @@
             device_id={"dom": peer}, device_id_type=pl.DeviceIdType.MESH))
     for m in scatter:
         m.start()
+    for k in range(pairs):
+        wide_ref[:, pair(k)] += dot(second_ref[:, pair(k)], map2[...])
+    out_ref[...] = wide_ref[:, c:].astype(BF16)
     got_ref[me] = pack_ref[me]
     arrive(scatter)
     total = got_ref[0]
@@ -396,7 +395,7 @@
     om_ref[0] = both[:, :c]
     om_ref[1] = both[:, c:]
     om_ref[2] = take(5 * c, c)[:, :c]
-    for m in scatter + final:
+    for m in round0 + round1 + round2 + round3 + scatter + final:
         m.wait_send()
 
 
@@ -421,7 +420,7 @@
                         pltpu.VMEM((128, 128), BF16), pltpu.VMEM((nodes, wide), BF16)],
         compiler_params=LIMIT,
         name="prepare",
-    )(cotangent[0], mix_weight, send_rows[0], counts, tile_cols, tile_vals)
+    )(cotangent[0].T, mix_weight, send_rows[0], counts, tile_cols, tile_vals)
     scaling = math.sqrt(float(windows * reps * nodes * parts * kept))
     unit = 8 * parts
     per = -(-6 * channels // unit) * unit // parts
@@ -431,7 +430,7 @@
                ((nodes, wide), BF16), ((nodes, wide), F32), ((nodes, flat), BF16),
                ((256, 256), BF16), ((128, 128), BF16), ((128, 128), BF16), ((128, 128), BF16),
                (conv_one.shape, F32), (conv_two.shape, F32), (mix_weight.shape, F32)]
-    scratch += [(blocks, BF16)] * 7
+    scratch += [((nodes, wide), F32)] + [(blocks, BF16)] * 7
     scratch += [((parts, per, BLK), F32), ((parts, per, BLK), F32), ((per, BLK), F32),
                 ((reps, per, BLK), F32), ((parts, per, BLK), F32)]
     dma = pltpu.SemaphoreType.DMA

time: 143 us -> 140 us (0.979)
  local copies, waits for them, and re-layouts: 7.42 us -> 5.56 us
    unnamed x12 -> x11, local copies, waits for them, and re-layouts: 7.42 us -> 5.56 us
where the time goes in v2:
time: 140 us
  Pallas kernels  134 us (96%)
  local copies, waits for them, and re-layouts  5.56 us (4%)
    pallas_call x1, Pallas kernels, shards(): pl.pallas_call(functools.partial(main_body, parts, reps, scaling), out_sh...  129 us
    unnamed x11, local copies, waits for them, and re-layouts  5.56 us
    pallas_call x1, Pallas kernels, shards(): pl.pallas_call(prepare_body, out_shape=[jax.ShapeDtypeStruct(s, d) for s,...  4.71 us

profile of v2, /device:TPU:0, one launch (start us, length us, event | category | flops | bytes accessed | tf_op | source)
XLA Modules:
  0.0 139.8 jit_solution(11909558071055290907)
XLA Ops:
  0.6 4.7 %prepare.1 = (bf16[256,1280]{1,0:T(8,128)(2,1)}, bf16[256,1024]{1,0:T(8,128)(2,1)}, bf16[256,640]{1,0:T(8,128)(2,1)}, f32[256,640]{1,0:T(8,128)}, bf16[8,640,128]{2,1,0:T(8,128)(2,1)}) custom-call(bf16[576,256]{1,0:T(8,128)(2,1)} %bitcast.10, bf16[3,64,64]{2,1,0:T(8,128)(2,1)} %mix_ref.3, s32[8,128]{1,0:T(8,128)} %bitcast.11, s32[1,8]{1,0:T(1,128)} %counts_ref.1, ...), custom_call_target="tpu_custom_call" | custom-call | tf_op jit(solution)/shard_map/prepare/pallas_call | solution.py:414
  5.3 128.9 %layer.1 = (bf16[256,576]{1,0:T(8,128)(2,1)}, bf16[256,768]{1,0:T(8,128)(2,1)}, f32[2,64,128]{2,1,0:T(8,128)}, f32[2,64,128]{2,1,0:T(8,128)}, f32[3,64,64]{2,1,0:T(8,128)}) custom-call(bf16[256,768]{1,0:T(8,128)(2,1)} %bitcast.8, bf16[256,640]{1,0:T(8,128)(2,1)} %get-tuple-element.15.cot_ref, bf16[2,64,128]{2,1,0:T(8,128)(2,1)} %conv1_ref.1, ...), custom_call_target="tpu_custom_call" | custom-call | tf_op jit(solution)/shard_map/layer/pallas_call | solution.py:437
  134.2 0.0 copy-start.2
  134.2 0.0 copy-start.1
  134.2 0.0 copy-start
  134.2 1.9 %copy.14 = bf16[1,256,576]{1,2,0:T(8,128)(2,1)} copy(bf16[1,256,576]{2,1,0:T(8,128)(2,1)} %bitcast.9) | data formatting | bytes 589824
  136.1 1.8 %copy.19 = bf16[1,256,768]{2,1,0:T(8,128)(2,1)} copy(bf16[1,256,768]{2,1,0:T(8,128)(2,1)} %bitcast.7) | data formatting | bytes 786432
  137.9 0.0 copy-done.2
  137.9 0.6 copy.20
  138.5 0.0 copy-done.1
  138.5 0.6 copy.21
  139.2 0.0 copy-done
  139.2 0.6 copy.22
Async XLA Ops:
  134.2 3.7 %copy-start.2 = (f32[2,64,128]{2,1,0:T(8,128)S(1)}, f32[2,64,128]{2,1,0:T(8,128)}, u32[]{:S(2)}) copy-start(f32[2,64,128]{2,1,0:T(8,128)} %get-tuple-element.37) | copy-start | bytes 196612
  134.2 4.3 %copy-start.1 = (f32[2,64,128]{2,1,0:T(8,128)S(1)}, f32[2,64,128]{2,1,0:T(8,128)}, u32[]{:S(2)}) copy-start(f32[2,64,128]{2,1,0:T(8,128)} %get-tuple-element.38) | copy-start | bytes 196612
  134.2 4.9 %copy-start = (f32[3,64,64]{2,1,0:T(8,128)S(1)}, f32[3,64,64]{2,1,0:T(8,128)}, u32[]{:S(2)}) copy-start(f32[3,64,64]{2,1,0:T(8,128)} %get-tuple-element.39) | copy-start | bytes 147460

commit v3 on v2

--- a/solution.py
+++ b/solution.py
@@ -232,7 +232,7 @@
 def main_body(parts, reps, scale,
               x_ref, cot_ref, conv1_ref, conv2_ref, mix_ref, dense_ref, picks_ref, base_ref,
               pieces_ref,
-              out_ref, grad_ref, o1_ref, o2_ref, om_ref,
+              out_ref, grad_ref, sum_ref,
               first_ref, hidden_ref, hop_ref, second_ref, up_ref, mid_ref, band_ref,
               map0, map1, map2, g1_ref, g2_ref, gm_ref,
               wide_ref, send1, send2, send3, recv0, recv1, recv2, recv3,
@@ -341,7 +341,7 @@
         m.start()
     for k in range(pairs):
         wide_ref[:, pair(k)] += dot(second_ref[:, pair(k)], map2[...])
-    out_ref[...] = wide_ref[:, c:].astype(BF16)
+    out_ref[...] = wide_ref[...].T[c:].astype(BF16)
     got_ref[me] = pack_ref[me]
     arrive(scatter)
     total = got_ref[0]
@@ -377,24 +377,7 @@
     sums_ref[me] = part_ref[...]
     arrive(final)
 
-    def take(first_row, rows):
-        found = []
-        done = 0
-        while done < rows:
-            slot, at = divmod(first_row + done, per)
-            step = min(per - at, rows - done)
-            found.append(sums_ref[slot, at : at + step, :])
-            done += step
-        return jnp.concatenate(found, axis=0) if len(found) > 1 else found[0]
-
-    o1_ref[0] = take(0, c)
-    o1_ref[1] = take(c, c)
-    o2_ref[0] = take(2 * c, c)
-    o2_ref[1] = take(3 * c, c)
-    both = take(4 * c, c)
-    om_ref[0] = both[:, :c]
-    om_ref[1] = both[:, c:]
-    om_ref[2] = take(5 * c, c)[:, :c]
+    sum_ref[...] = sums_ref[...]
     for m in round0 + round1 + round2 + round3 + scatter + final:
         m.wait_send()
 
@@ -424,8 +407,7 @@
     scaling = math.sqrt(float(windows * reps * nodes * parts * kept))
     unit = 8 * parts
     per = -(-6 * channels // unit) * unit // parts
-    results = [((nodes, kept * channels), BF16), ((nodes, flat), BF16), (conv_one.shape, F32),
-               (conv_two.shape, F32), (mix_weight.shape, F32)]
+    results = [((kept * channels, nodes), BF16), ((nodes, flat), BF16), ((parts, per, BLK), F32)]
     scratch = [((nodes, flat), BF16), ((nodes, wide), BF16), ((nodes, wide), BF16),
                ((nodes, wide), BF16), ((nodes, wide), F32), ((nodes, flat), BF16),
                ((256, 256), BF16), ((128, 128), BF16), ((128, 128), BF16), ((128, 128), BF16),
@@ -434,11 +416,11 @@
     scratch += [((parts, per, BLK), F32), ((parts, per, BLK), F32), ((per, BLK), F32),
                 ((reps, per, BLK), F32), ((parts, per, BLK), F32)]
     dma = pltpu.SemaphoreType.DMA
-    output, grad_input, g1, g2, gm = pl.pallas_call(
+    output, grad_input, packed = pl.pallas_call(
         functools.partial(main_body, parts, reps, scaling),
         out_shape=[jax.ShapeDtypeStruct(s, d) for s, d in results],
         in_specs=[VM] * 9,
-        out_specs=[VM] * 5,
+        out_specs=[VM] * 3,
         scratch_shapes=[pltpu.VMEM(s, d) for s, d in scratch]
         + [dma((4, parts)), dma((4, parts)), dma((2, parts)), dma((2, parts)), dma((reps,)),
            dma((reps,))],
@@ -446,7 +428,16 @@
             vmem_limit_bytes=60 * 1024 * 1024, collective_id=0, has_side_effects=True),
         name="layer",
     )(inputs[0], cot_wide, conv_one, conv_two, mix_weight, dense, picks, base, pieces)
-    return output[None], grad_input[None], g1, g2, gm
+    c = channels
+    rows = packed.reshape(parts * per, BLK)
+    gm = jnp.stack([rows[4 * c : 5 * c, :c], rows[4 * c : 5 * c, c:], rows[5 * c : 6 * c, :c]])
+    return (
+        output.T[None],
+        grad_input[None],
+        rows[: 2 * c].reshape(conv_one.shape),
+        rows[2 * c : 4 * c].reshape(conv_two.shape),
+        gm,
+    )
 
 
 def solution(mesh):

time: 140 us -> 140 us (level)
    unnamed x11 -> x4, local copies, waits for them, and re-layouts: 5.56 us -> 2.44 us
    slice x0 -> x1, local copies, waits for them, and re-layouts: none -> 1.53 us  [shards(): rows[2 * c:4 * c].reshape(conv_two.shape)]
where the time goes in v3:
time: 140 us
  Pallas kernels  133 us (95%)
  local copies, waits for them, and re-layouts  4.89 us (3%)
    pallas_call x1, Pallas kernels, shards(): pl.pallas_call(functools.partial(main_body, parts, reps, scaling), out_sh...  129 us
    pallas_call x1, Pallas kernels, shards(): pl.pallas_call(prepare_body, out_shape=[jax.ShapeDtypeStruct(s, d) for s,...  4.71 us

profile of v3, /device:TPU:0, one launch (start us, length us, event | category | flops | bytes accessed | tf_op | source)
XLA Modules:
  0.0 139.6 jit_solution(18242080082035221224)
XLA Ops:
  0.6 4.7 %prepare.1 = (bf16[256,1280]{1,0:T(8,128)(2,1)}, bf16[256,1024]{1,0:T(8,128)(2,1)}, bf16[256,640]{1,0:T(8,128)(2,1)}, f32[256,640]{1,0:T(8,128)}, bf16[8,640,128]{2,1,0:T(8,128)(2,1)}) custom-call(bf16[576,256]{1,0:T(8,128)(2,1)} %bitcast.20, bf16[3,64,64]{2,1,0:T(8,128)(2,1)} %mix_ref.3, s32[8,128]{1,0:T(8,128)} %bitcast.26, s32[1,8]{1,0:T(1,128)} %counts_ref.1, ...), custom_call_target="tpu_custom_call" | custom-call | tf_op jit(solution)/shard_map/prepare/pallas_call | solution.py:397
  5.3 128.7 %layer.1 = (bf16[576,256]{1,0:T(8,128)(2,1)}, bf16[256,768]{1,0:T(8,128)(2,1)}, f32[8,48,128]{2,1,0:T(8,128)}) custom-call(bf16[256,768]{1,0:T(8,128)(2,1)} %bitcast.19, bf16[256,640]{1,0:T(8,128)(2,1)} %get-tuple-element.13.cot_ref, bf16[2,64,128]{2,1,0:T(8,128)(2,1)} %conv1_ref.1, bf16[2,64,128]{2,1,0:T(8,128)(2,1)} %conv2_ref.1, ...), custom_call_target="tpu_custom_call" | custom-call | tf_op jit(solution)/shard_map/layer/pallas_call | solution.py:419
  134.1 0.0 copy-start
  134.1 0.9 slice_bitcast_fusion.2
  135.0 1.5 %fusion = (f32[128,128]{1,0:T(8,128)}, f32[128,128]{1,0:T(8,128)}) fusion(f32[384,128]{1,0:T(8,128)} %bitcast.23), kind=kLoop, calls=%fused_computation.4 | loop fusion | bytes 262144 | tf_op jit(solution)/shard_map/slice | solution.py:438
  136.5 0.6 pad_maximum_fusion
  137.2 1.7 %copy.16 = bf16[1,256,576]{1,2,0:T(8,128)(2,1)} copy(bf16[1,256,576]{1,2,0:T(8,128)(2,1)} %bitcast.21) | data formatting | bytes 589824
  138.9 0.0 copy-done
  138.9 0.7 copy.17
Async XLA Ops:
  134.1 4.8 %copy-start = (bf16[256,768]{1,0:T(8,128)(2,1)S(1)}, bf16[256,768]{1,0:T(8,128)(2,1)}, u32[]{:S(2)}) copy-start(bf16[256,768]{1,0:T(8,128)(2,1)} %get-tuple-element.19) | copy-start | bytes 1179652
